TPU v7x, 32 devices: a whole 2x2x4 slice. The times are simulated.
32 devices in a mesh: blk: 4 (over y, x), dom: 8 (over z, core).
Axes of the slice: x: 2, y: 2, z: 4, core: 2. Of those that a mesh axis runs over, the one named last changes fastest.
Arguments:
- orbitals: float32 [4, 64, 256, 256], P('blk', 'dom'), may hold values from -7 to 7
- dielectric: float32 [64, 256, 256], P('dom'), may hold values from 1 to 10
Outputs:
- exchange: float32 [4, 64, 256, 256], P('blk', 'dom')
All inputs are finite; a program needn't handle non-finite values.
Results may differ from a plain program's by a relative error of at most 0.0001.
Values sent between devices are 32-bit elements; how exact they have to be, the bound alone decides.
No kernel may reach another device: no remote copies, remote signals or barrier semaphores. Data moves between devices by JAX's collectives and lax.ppermute only.
A program may use at most 128 MiB of HBM per device.

v0:
```python
import math

import jax
import jax.numpy as jnp
from jax import lax
from jax.sharding import PartitionSpec as P

ITERS = 3


FOUR_PI = 4.0 * math.pi


def padded_2(cells, sides, width):
    for axis, dim in sides:
        count = lax.axis_size(axis)
        ends = count - 1
        head = lax.slice_in_dim(cells, 0, width, axis=dim)
        tail = lax.slice_in_dim(cells, cells.shape[dim] - width, cells.shape[dim], axis=dim)
        cells = jnp.concatenate(
            [
                lax.ppermute(tail, axis, [(i, (i + 1) % count) for i in range(ends)]),
                cells,
                lax.ppermute(head, axis, [((i + 1) % count, i) for i in range(ends)]),
            ],
            axis=dim,
        )
    return cells


def shifted(value, axis, steps):
    count = lax.axis_size(axis)
    pairs = [(source, (source + steps) % count) for source in range(count)]
    return lax.ppermute(value, axis, pairs)


def face_weights(eps_pad):
    center = eps_pad[1:-1, 1:-1, 1:-1]
    return (
        (center + eps_pad[2:, 1:-1, 1:-1]) * 0.5,
        (center + eps_pad[:-2, 1:-1, 1:-1]) * 0.5,
        (center + eps_pad[1:-1, 2:, 1:-1]) * 0.5,
        (center + eps_pad[1:-1, :-2, 1:-1]) * 0.5,
        (center + eps_pad[1:-1, 1:-1, 2:]) * 0.5,
        (center + eps_pad[1:-1, 1:-1, :-2]) * 0.5,
    )


def apply_operator(field_in, weights):
    padded = padded_2(field_in, (("dom", 1),), 1)
    padded = jnp.pad(padded, ((0, 0), (0, 0), (1, 1), (1, 1)))
    center = padded[:, 1:-1, 1:-1, 1:-1]
    result = weights[0] * (center - padded[:, 2:, 1:-1, 1:-1])
    result = result + weights[1] * (center - padded[:, :-2, 1:-1, 1:-1])
    result = result + weights[2] * (center - padded[:, 1:-1, 2:, 1:-1])
    result = result + weights[3] * (center - padded[:, 1:-1, :-2, 1:-1])
    result = result + weights[4] * (center - padded[:, 1:-1, 1:-1, 2:])
    result = result + weights[5] * (center - padded[:, 1:-1, 1:-1, :-2])
    return result


def shaped(values):
    return values.reshape(values.shape[0], 1, 1, 1)


def local_inner(first, second):
    return jnp.sum(first * second, axis=(1, 2, 3))


def squares(residual):
    return shaped(lax.psum(local_inner(residual, residual), "dom"))


def solve_poisson(right_side, weights):
    solution = jnp.zeros_like(right_side)
    residual = right_side
    direction = right_side
    norm_now = squares(residual)
    for iteration in range(ITERS):
        applied = apply_operator(direction, weights)
        curved = shaped(lax.psum(local_inner(direction, applied), "dom"))
        step_length = norm_now / curved
        solution = solution + step_length * direction
        residual = residual - step_length * applied
        norm_next = squares(residual)
        direction = residual + norm_next / norm_now * direction
        norm_now = norm_next
    return solution


def per_device(orbitals, dielectric):
    eps_pad = padded_2(dielectric, (("dom", 0),), 1)
    eps_pad = jnp.pad(eps_pad, ((0, 0), (1, 1), (1, 1)))
    weights = face_weights(eps_pad)
    left_orbital = shifted(orbitals, "blk", 1)
    density = FOUR_PI * orbitals * left_orbital
    potential = solve_poisson(density, weights)
    returned = shifted(potential * orbitals, "blk", -1)
    exchange = -(potential * left_orbital + returned)
    return exchange


def solution(mesh):
    return jax.shard_map(
        per_device,
        mesh=mesh,
        in_specs=(P("blk", "dom", None, None), P("dom", None, None)),
        out_specs=P("blk", "dom", None, None),
        check_vma=False,
    )
```

profile of v0, /device:TPU:0, one launch (start us, length us, event | category | flops | bytes accessed | tf_op | source)
XLA Modules:
  0.0 248.8 jit_solution(14998920902760468024)
XLA Ops:
  0.0 3.0 %collective-permute-start = (f32[1,8,256,256]{3,2,1,0:T(8,128)}, f32[1,8,256,256]{3,2,1,0:T(8,128)S(1)}, u32[]{:S(2)}, u32[]{:S(2)}) collective-permute-start(f32[1,8,256,256]{3,2,1,0:T(8,128)} %param.2), channel_id=1, source_target_pairs={{0,8},{8,16},{16,24},{24,0},{1,9},{9,17},{17,25},{25,1},{2,10},{10... | collective-permute-start | bytes 6291464 | tf_op jit(solution)/shard_map/ppermute | solution.py:34
  3.0 1.1 fusion.66
  4.0 1.5 collective-permute-start.3
  5.5 1.3 collective-permute-start.1
  6.8 42.9 %collective-permute-done = f32[1,8,256,256]{3,2,1,0:T(8,128)S(1)} collective-permute-done((f32[1,8,256,256]{3,2,1,0:T(8,128)}, f32[1,8,256,256]{3,2,1,0:T(8,128)S(1)}, u32[]{:S(2)}, u32[]{:S(2)}) %collective-permute-start) | collective-permute-done | bytes 2097184 | tf_op jit(solution)/shard_map/ppermute | solution.py:34
  49.8 0.0 copy-start.9
  49.8 0.0 copy-start.5
  49.8 2.7 %multiply_multiply_fusion = f32[1,8,256,256]{3,2,1,0:T(8,128)S(1)} fusion(f32[1,8,256,256]{3,2,1,0:T(8,128)S(1)} %collective-permute-done, f32[1,8,256,256]{3,2,1,0:T(8,128)} %param.2), kind=kLoop, calls=%fused_computation.112 | loop fusion | flops 1048576 | bytes 6291456 | tf_op jit(solution)/shard_map/mul | solution.py:96
  52.4 0.0 copy-done.9
  52.5 1.3 collective-permute-start.4
  53.8 1.3 collective-permute-start.2
  55.1 0.0 collective-permute-done.3
  55.1 0.0 collective-permute-done.1
  55.1 0.0 copy-done.5
  55.1 2.9 %select_maximum_fusion.6 = f32[10,258,258]{2,1,0:T(8,128)S(1)} fusion(f32[1,256,256]{2,1,0:T(8,128)S(1)} %collective-permute-done.1, f32[8,256,256]{2,1,0:T(8,128)S(1)} %copy-done.5, f32[1,256,256]{2,1,0:T(8,128)S(1)} %collective-permute-done.3), kind=kLoop, calls=%fused_computation.14 | loop fusion | flops 9984600 | bytes 5284000 | tf_op jit(solution)/shard_map/concatenate | solution.py:20
  58.1 0.0 copy-start
  58.1 0.0 collective-permute-done.4
  58.1 1.1 collective-permute-done.2
  59.2 2.9 %select_maximum_fusion.4 = f32[1,10,258,258]{3,2,1,0:T(8,128)S(1)} fusion(f32[1,1,256,256]{3,2,1,0:T(8,128)S(1)} %collective-permute-done.2, f32[1,8,256,256]{3,2,1,0:T(8,128)S(1)} %multiply_multiply_fusion, f32[1,1,256,256]{3,2,1,0:T(8,128)S(1)} %collective-permute-done.4), kind=kLoop, calls=%fused_computation.12 | loop fusion | flops 9984600 | bytes 5284000 | tf_op jit(solution)/shard_map/concatenate | solution.py:20
  62.2 0.0 copy-done
  62.2 6.2 %multiply_reduce_fusion.3 = (f32[]{:T(128)}, f32[]{:T(128)}, f32[1,8,256,256]{3,2,1,0:T(8,128)}) fusion(f32[1,8,256,256]{3,2,1,0:T(8,128)S(1)} %multiply_multiply_fusion, f32[1,10,258,258]{3,2,1,0:T(8,128)S(1)} %select_maximum_fusion.4, f32[8,256,256]{2,1,0:T(8,128)S(1)} %copy-done.5, f32[10,258,258]{2,1,0:T(8,128)S(1)} %select_maximum_fusion.6, ...), kind=kLoop, calls=%fused_computation.110 | loop fusion | flops 19398656 | bytes 24117256 | tf_op jit(solution)/shard_map/reduce_sum | solution.py:67
  68.3 19.0 %all-reduce.4 = (f32[1]{0:T(128)}, f32[1]{0:T(128)}) all-reduce(f32[1]{0:T(128)} %bitcast, f32[1]{0:T(128)} %bitcast.7), channel_id=1, replica_groups=mesh['blk'=4,'dom'=8] {'dom'}, use_global_device_ids=true, to_apply=%region_1.2 | all-reduce | flops 2 | bytes 16 | tf_op jit(solution)/shard_map/psum | solution.py:71
  88.6 2.8 %multiply_reduce_fusion.2 = f32[]{:T(128)} fusion(f32[1,8,256,256]{3,2,1,0:T(8,128)S(1)} %multiply_multiply_fusion, f32[1,8,256,256]{3,2,1,0:T(8,128)} %get-tuple-element.13, f32[]{:T(128)} %bitcast.8), kind=kLoop, calls=%fused_computation.108 | loop fusion | flops 2097151 | bytes 4194312 | tf_op jit(solution)/shard_map/reduce_sum | solution.py:67
  91.3 14.2 %psum.44 = f32[1]{0:T(128)} all-reduce(f32[1]{0:T(128)} %bitcast.9), channel_id=1, replica_groups=mesh['blk'=4,'dom'=8] {'dom'}, use_global_device_ids=true, to_apply=%region_5.6 | all-reduce | flops 1 | bytes 8 | tf_op jit(solution)/shard_map/psum | solution.py:71
  106.7 1.9 multiply_add_fusion.2
  108.5 0.0 copy-start.3
  108.6 1.8 collective-permute-start.6
  110.4 0.0 copy-start.1
  110.4 0.0 copy-start.6
  110.4 1.6 collective-permute-start.5
  112.0 0.0 collective-permute-done.6
  112.0 2.1 collective-permute-done.5
  114.1 2.9 %select_maximum_fusion.2 = f32[1,10,258,258]{3,2,1,0:T(8,128)S(1)} fusion(f32[1,1,256,256]{3,2,1,0:T(8,128)S(1)} %collective-permute-done.5, f32[1,8,256,256]{3,2,1,0:T(8,128)S(1)} %multiply_add_fusion.2, f32[1,1,256,256]{3,2,1,0:T(8,128)S(1)} %collective-permute-done.6), kind=kLoop, calls=%fused_computation.10 | loop fusion | flops 9984600 | bytes 5284000 | tf_op jit(solution)/shard_map/concatenate | solution.py:20
  117.1 0.0 copy-done.3
  117.1 0.0 copy-done.1
  117.1 0.0 copy-done.6
  117.1 6.4 %multiply_reduce_fusion.1 = (f32[]{:T(128)}, f32[1,8,256,256]{3,2,1,0:T(8,128)}) fusion(f32[1,8,256,256]{3,2,1,0:T(8,128)S(1)} %multiply_add_fusion.2, f32[1,10,258,258]{3,2,1,0:T(8,128)S(1)} %select_maximum_fusion.2, f32[8,256,256]{2,1,0:T(8,128)S(1)} %copy-done.6, f32[10,258,258]{2,1,0:T(8,128)S(1)} %copy-done.1, ...), kind=kLoop, calls=%fused_computation.106 | loop fusion | flops 18350080 | bytes 24117252 | tf_op jit(solution)/shard_map/reduce_sum | solution.py:67
  123.5 18.5 %psum.45 = f32[1]{0:T(128)} all-reduce(f32[1]{0:T(128)} %bitcast.11), channel_id=1, replica_groups=mesh['blk'=4,'dom'=8] {'dom'}, use_global_device_ids=true, to_apply=%region_7.8 | all-reduce | flops 1 | bytes 8 | tf_op jit(solution)/shard_map/psum | solution.py:81
  143.1 4.6 %multiply_reduce_fusion = (f32[]{:T(128)}, f32[1,8,256,256]{3,2,1,0:T(8,128)}) fusion(f32[1,8,256,256]{3,2,1,0:T(8,128)} %get-tuple-element.12, f32[]{:T(128)} %bitcast.12, f32[1,8,256,256]{3,2,1,0:T(8,128)S(1)} %multiply_multiply_fusion, f32[1,8,256,256]{3,2,1,0:T(8,128)} %get-tuple-element.13, f32[]{:T(128)} %bitcast.8), kind=kLoop, calls=%fused_computation.104 | loop fusion | flops 3145727 | bytes 8388620 | tf_op jit(solution)/shard_map/reduce_sum | solution.py:67
  147.8 14.2 %psum.46 = f32[1]{0:T(128)} all-reduce(f32[1]{0:T(128)} %bitcast.13), channel_id=1, replica_groups=mesh['blk'=4,'dom'=8] {'dom'}, use_global_device_ids=true, to_apply=%region_9.10 | all-reduce | flops 1 | bytes 8 | tf_op jit(solution)/shard_map/psum | solution.py:71
  163.2 2.5 %multiply_add_fusion.1 = f32[1,8,256,256]{3,2,1,0:T(8,128)S(1)} fusion(f32[1,8,256,256]{3,2,1,0:T(8,128)} %get-tuple-element.10, f32[1,8,256,256]{3,2,1,0:T(8,128)} %copy-done.3, f32[]{:T(128)} %bitcast.14), kind=kLoop, calls=%fused_computation.103 | loop fusion | flops 1048576 | bytes 6291460 | tf_op jit(solution)/shard_map/add | solution.py:86
  165.7 1.8 collective-permute-start.8
  167.5 0.0 copy-start.2
  167.5 0.0 copy-start.7
  167.6 1.7 collective-permute-start.7
  169.3 0.0 collective-permute-done.8
  169.3 1.9 collective-permute-done.7
  171.2 2.9 %select_maximum_fusion = f32[1,10,258,258]{3,2,1,0:T(8,128)S(1)} fusion(f32[1,1,256,256]{3,2,1,0:T(8,128)S(1)} %collective-permute-done.7, f32[1,8,256,256]{3,2,1,0:T(8,128)S(1)} %multiply_add_fusion.1, f32[1,1,256,256]{3,2,1,0:T(8,128)S(1)} %collective-permute-done.8), kind=kLoop, calls=%fused_computation.8 | loop fusion | flops 9984600 | bytes 5284000 | tf_op jit(solution)/shard_map/concatenate | solution.py:20
  174.2 0.0 copy-done.2
  174.2 0.0 copy-done.7
  174.2 5.5 %fusion.9 = f32[]{:T(128)} fusion(f32[1,8,256,256]{3,2,1,0:T(8,128)S(1)} %multiply_add_fusion.1, f32[1,10,258,258]{3,2,1,0:T(8,128)S(1)} %select_maximum_fusion, f32[1,1,256,256]{3,2,1,0:T(8,128)S(1)} %collective-permute-done.8, f32[1,1,256,256]{3,2,1,0:T(8,128)S(1)} %collective-permute-done.7, f32[8,256,256]{2,1,0:T(8,128)S(1)} %copy-done.7, ...), kind=kLoop, calls=%fused_computation.26 | loop fusion | flops 18350080 | bytes 22020100 | tf_op jit(solution)/shard_map/reduce_sum | solution.py:67
  179.6 18.5 %psum.47 = f32[1]{0:T(128)} all-reduce(f32[1]{0:T(128)} %bitcast.15), channel_id=1, replica_groups=mesh['blk'=4,'dom'=8] {'dom'}, use_global_device_ids=true, to_apply=%region_11.12 | all-reduce | flops 1 | bytes 8 | tf_op jit(solution)/shard_map/psum | solution.py:81
  199.5 0.0 copy-start.4
  199.5 0.0 copy-start.8
  199.5 0.0 copy-start.10
  199.5 3.6 %fusion.61 = f32[1,8,256,256]{3,2,1,0:T(8,128)S(1)} fusion(f32[1,8,256,256]{3,2,1,0:T(8,128)} %param.2, f32[]{:T(128)} %bitcast.16, f32[1,8,256,256]{3,2,1,0:T(8,128)} %copy-done.3, f32[1,8,256,256]{3,2,1,0:T(8,128)S(1)} %multiply_multiply_fusion, f32[1,8,256,256]{3,2,1,0:T(8,128)} %get-tuple-element.10, f32[]{:T(128)} %bitcast.14, f32[]{:T(128)} %bitcast.12, ...), kind=kLoop, calls=%fused_computation.113 | loop fusion | flops 4194304 | bytes 10485776 | tf_op jit(solution)/shard_map/mul | solution.py:98
  203.1 1.6 collective-permute-start.9
  204.7 41.9 %collective-permute-done.9 = f32[1,8,256,256]{3,2,1,0:T(8,128)S(1)} collective-permute-done((f32[1,8,256,256]{3,2,1,0:T(8,128)S(1)}, f32[1,8,256,256]{3,2,1,0:T(8,128)S(1)}, u32[]{:S(2)}, u32[]{:S(2)}) %collective-permute-start.9) | collective-permute-done | bytes 2097184 | tf_op jit(solution)/shard_map/ppermute | solution.py:34
  246.6 0.0 copy-done.4
  246.6 0.0 copy-done.8
  246.6 0.0 copy-done.10
  246.6 2.3 add_negate_fusion
  (3 shorter events, 0.1 us)
Async XLA Ops:
  0.0 49.8 %collective-permute-start = (f32[1,8,256,256]{3,2,1,0:T(8,128)}, f32[1,8,256,256]{3,2,1,0:T(8,128)S(1)}, u32[]{:S(2)}, u32[]{:S(2)}) collective-permute-start(f32[1,8,256,256]{3,2,1,0:T(8,128)} %param.2), channel_id=1, source_target_pairs={{0,8},{8,16},{16,24},{24,0},{1,9},{9,17},{17,25},{25,1},{2,10},{10... | collective-permute-start | bytes 6291464 | tf_op jit(solution)/shard_map/ppermute | solution.py:34
  4.0 51.1 %collective-permute-start.3 = (f32[1,256,256]{2,1,0:T(8,128)S(1)}, f32[1,256,256]{2,1,0:T(8,128)S(1)}, u32[]{:S(2)}, u32[]{:S(2)}) collective-permute-start(f32[1,256,256]{2,1,0:T(8,128)S(1)} %get-tuple-element.18), channel_id=1, source_target_pairs={{0,1},{1,2},{2,3},{3,4},{4,5},{5,6},{6,7},{8,9},{9,10},{10,11},{11... | collective-permute-start | bytes 786440 | tf_op jit(solution)/shard_map/ppermute | solution.py:22
  5.5 49.6 %collective-permute-start.1 = (f32[1,256,256]{2,1,0:T(8,128)S(1)}, f32[1,256,256]{2,1,0:T(8,128)S(1)}, u32[]{:S(2)}, u32[]{:S(2)}) collective-permute-start(f32[1,256,256]{2,1,0:T(8,128)S(1)} %get-tuple-element.19), channel_id=1, source_target_pairs={{1,0},{2,1},{3,2},{4,3},{5,4},{6,5},{7,6},{9,8},{10,9},{11,10},{12... | collective-permute-start | bytes 786440 | tf_op jit(solution)/shard_map/ppermute | solution.py:24
  49.8 2.7 %copy-start.9 = (f32[1,8,256,256]{3,2,1,0:T(8,128)}, f32[1,8,256,256]{3,2,1,0:T(8,128)S(1)}, u32[]{:S(2)}) copy-start(f32[1,8,256,256]{3,2,1,0:T(8,128)S(1)} %collective-permute-done) | copy-start | bytes 6291460
  49.8 5.4 %copy-start.5 = (f32[8,256,256]{2,1,0:T(8,128)S(1)}, f32[8,256,256]{2,1,0:T(8,128)}, u32[]{:S(2)}) copy-start(f32[8,256,256]{2,1,0:T(8,128)} %param.3) | copy-start | bytes 6291460
  52.5 5.6 %collective-permute-start.4 = (f32[1,1,256,256]{3,2,1,0:T(8,128)S(1)}, f32[1,1,256,256]{3,2,1,0:T(8,128)S(1)}, u32[]{:S(2)}, u32[]{:S(2)}) collective-permute-start(f32[1,1,256,256]{3,2,1,0:T(8,128)S(1)} %get-tuple-element.20), channel_id=1, source_target_pairs={{0,1},{1,2},{2,3},{3,4},{4,5},{5,6},{6,7},{8,9},{9,10},{10,11},{11... | collective-permute-start | bytes 786440 | tf_op jit(solution)/shard_map/ppermute | solution.py:22
  53.8 5.4 %collective-permute-start.2 = (f32[1,1,256,256]{3,2,1,0:T(8,128)S(1)}, f32[1,1,256,256]{3,2,1,0:T(8,128)S(1)}, u32[]{:S(2)}, u32[]{:S(2)}) collective-permute-start(f32[1,1,256,256]{3,2,1,0:T(8,128)S(1)} %get-tuple-element.21), channel_id=1, source_target_pairs={{1,0},{2,1},{3,2},{4,3},{5,4},{6,5},{7,6},{9,8},{10,9},{11,10},{12... | collective-permute-start | bytes 786440 | tf_op jit(solution)/shard_map/ppermute | solution.py:24
  58.1 4.1 %copy-start = (f32[10,258,258]{2,1,0:T(8,128)}, f32[10,258,258]{2,1,0:T(8,128)S(1)}, u32[]{:S(2)}) copy-start(f32[10,258,258]{2,1,0:T(8,128)S(1)} %select_maximum_fusion.6) | copy-start | bytes 7987684
  108.5 8.5 %copy-start.3 = (f32[1,8,256,256]{3,2,1,0:T(8,128)}, f32[1,8,256,256]{3,2,1,0:T(8,128)S(1)}, u32[]{:S(2)}) copy-start(f32[1,8,256,256]{3,2,1,0:T(8,128)S(1)} %multiply_add_fusion.2) | copy-start | bytes 6291460
  108.6 3.4 %collective-permute-start.6 = (f32[1,1,256,256]{3,2,1,0:T(8,128)S(1)}, f32[1,1,256,256]{3,2,1,0:T(8,128)S(1)}, u32[]{:S(2)}, u32[]{:S(2)}) collective-permute-start(f32[1,1,256,256]{3,2,1,0:T(8,128)S(1)} %get-tuple-element.16), channel_id=1, source_target_pairs={{0,1},{1,2},{2,3},{3,4},{4,5},{5,6},{6,7},{8,9},{9,10},{10,11},{11... | collective-permute-start | bytes 786440 | tf_op jit(solution)/shard_map/ppermute | solution.py:22
  110.4 6.6 %copy-start.1 = (f32[10,258,258]{2,1,0:T(8,128)S(1)}, f32[10,258,258]{2,1,0:T(8,128)}, u32[]{:S(2)}) copy-start(f32[10,258,258]{2,1,0:T(8,128)} %copy-done) | copy-start | bytes 7987684
  110.4 6.6 %copy-start.6 = (f32[8,256,256]{2,1,0:T(8,128)S(1)}, f32[8,256,256]{2,1,0:T(8,128)}, u32[]{:S(2)}) copy-start(f32[8,256,256]{2,1,0:T(8,128)} %param.3) | copy-start | bytes 6291460
  110.4 3.7 %collective-permute-start.5 = (f32[1,1,256,256]{3,2,1,0:T(8,128)S(1)}, f32[1,1,256,256]{3,2,1,0:T(8,128)S(1)}, u32[]{:S(2)}, u32[]{:S(2)}) collective-permute-start(f32[1,1,256,256]{3,2,1,0:T(8,128)S(1)} %get-tuple-element.17), channel_id=1, source_target_pairs={{1,0},{2,1},{3,2},{4,3},{5,4},{6,5},{7,6},{9,8},{10,9},{11,10},{12... | collective-permute-start | bytes 786440 | tf_op jit(solution)/shard_map/ppermute | solution.py:24
  165.7 3.6 %collective-permute-start.8 = (f32[1,1,256,256]{3,2,1,0:T(8,128)S(1)}, f32[1,1,256,256]{3,2,1,0:T(8,128)S(1)}, u32[]{:S(2)}, u32[]{:S(2)}) collective-permute-start(f32[1,1,256,256]{3,2,1,0:T(8,128)S(1)} %get-tuple-element.14), channel_id=1, source_target_pairs={{0,1},{1,2},{2,3},{3,4},{4,5},{5,6},{6,7},{8,9},{9,10},{10,11},{11... | collective-permute-start | bytes 786440 | tf_op jit(solution)/shard_map/ppermute | solution.py:22
  167.5 6.6 %copy-start.2 = (f32[10,258,258]{2,1,0:T(8,128)S(1)}, f32[10,258,258]{2,1,0:T(8,128)}, u32[]{:S(2)}) copy-start(f32[10,258,258]{2,1,0:T(8,128)} %copy-done) | copy-start | bytes 7987684
  167.5 6.6 %copy-start.7 = (f32[8,256,256]{2,1,0:T(8,128)S(1)}, f32[8,256,256]{2,1,0:T(8,128)}, u32[]{:S(2)}) copy-start(f32[8,256,256]{2,1,0:T(8,128)} %param.3) | copy-start | bytes 6291460
  167.6 3.7 %collective-permute-start.7 = (f32[1,1,256,256]{3,2,1,0:T(8,128)S(1)}, f32[1,1,256,256]{3,2,1,0:T(8,128)S(1)}, u32[]{:S(2)}, u32[]{:S(2)}) collective-permute-start(f32[1,1,256,256]{3,2,1,0:T(8,128)S(1)} %get-tuple-element.15), channel_id=1, source_target_pairs={{1,0},{2,1},{3,2},{4,3},{5,4},{6,5},{7,6},{9,8},{10,9},{11,10},{12... | collective-permute-start | bytes 786440 | tf_op jit(solution)/shard_map/ppermute | solution.py:24
  199.5 47.1 %copy-start.4 = (f32[1,8,256,256]{3,2,1,0:T(8,128)S(1)}, f32[1,8,256,256]{3,2,1,0:T(8,128)}, u32[]{:S(2)}) copy-start(f32[1,8,256,256]{3,2,1,0:T(8,128)} %copy-done.3) | copy-start | bytes 6291460
  199.5 47.1 %copy-start.8 = (f32[1,8,256,256]{3,2,1,0:T(8,128)S(1)}, f32[1,8,256,256]{3,2,1,0:T(8,128)}, u32[]{:S(2)}) copy-start(f32[1,8,256,256]{3,2,1,0:T(8,128)} %get-tuple-element.10) | copy-start | bytes 6291460
  199.5 47.1 %copy-start.10 = (f32[1,8,256,256]{3,2,1,0:T(8,128)S(1)}, f32[1,8,256,256]{3,2,1,0:T(8,128)}, u32[]{:S(2)}) copy-start(f32[1,8,256,256]{3,2,1,0:T(8,128)} %copy-done.9) | copy-start | bytes 6291460
  203.1 43.5 %collective-permute-start.9 = (f32[1,8,256,256]{3,2,1,0:T(8,128)S(1)}, f32[1,8,256,256]{3,2,1,0:T(8,128)S(1)}, u32[]{:S(2)}, u32[]{:S(2)}) collective-permute-start(f32[1,8,256,256]{3,2,1,0:T(8,128)S(1)} %fusion.61), channel_id=1, source_target_pairs={{0,24},{8,0},{16,8},{24,16},{1,25},{9,1},{17,9},{25,17},{2,26},{10... | collective-permute-start | bytes 6291464 | tf_op jit(solution)/shard_map/ppermute | solution.py:34
where the time goes:
time: 249 us
  waiting for transfers between devices  90 us (36%)
  blocking collectives  84.4 us (34%)
  other arithmetic  50 us (20%)
  starting transfers between devices  16.8 us (7%)
  between operations  6.38 us (3%)
    ppermute x2, waiting for transfers between devices, shifted(): return lax.ppermute(value, axis, pairs)  84.8 us
    psum x3, blocking collectives, squares(): return shaped(lax.psum(local_inner(residual, residual), 'dom'))  47.4 us
    psum x2, blocking collectives, solve_poisson(): curved = shaped(lax.psum(local_inner(direction, applied), 'dom'))  37 us
    reduce_sum x5, other arithmetic, local_inner(): return jnp.sum(first * second, axis=(1, 2, 3))  25.4 us
    concatenate x4, other arithmetic, padded_2(): jnp.concatenate([lax.ppermute(tail, axis, [(i, (i + 1) % count) for i in...  11.7 us
    ppermute x4, starting transfers between devices, padded_2(): lax.ppermute(tail, axis, [(i, (i + 1) % count) for i in range(ends)])  6.4 us
    ppermute x4, starting transfers between devices, padded_2(): lax.ppermute(head, axis, [((i + 1) % count, i) for i in range(ends)])  5.88 us
    ppermute x4, waiting for transfers between devices, padded_2(): lax.ppermute(head, axis, [((i + 1) % count, i) for i in range(ends)])  5.19 us
  transfers between devices with their start and end apart: 10, of which 5 were waited for; matrix products, arithmetic and copies ran while one was open for 3% of the time, Pallas kernels for 0%

commit v1 on v0

v1 whole, which is shorter than its diff:
```python
import functools
import math

import jax
import jax.numpy as jnp
from jax import lax
from jax.experimental import pallas as pl
from jax.experimental.pallas import tpu as pltpu
from jax.sharding import PartitionSpec as P

FOUR_PI = 4.0 * math.pi
TILE = 8
LEFT = 2
RIGHT = 3
MOMENTS = 6
VMEM = pl.BlockSpec(memory_space=pltpu.VMEM)
SMEM = pl.BlockSpec(memory_space=pltpu.SMEM)


def roles(rows, window):
    odd = lax.rem(lax.axis_index("blk"), 2)
    upper = rows - window
    return (1 - odd) * upper, odd * upper


def edges():
    at = lax.axis_index("dom")
    last = lax.axis_size("dom") - 1
    return jnp.minimum(at, 1), jnp.minimum(last - at, 1)


def tile_rows(tile):
    return slice(tile * TILE, (tile + 1) * TILE)


def window_rows(start, tile):
    return pl.ds(pl.multiple_of(start + tile * TILE, TILE), TILE)


def next_lane(value):
    return pltpu.roll(value, value.shape[1] - 1, 1)


def prev_lane(value):
    return pltpu.roll(value, 1, 1)


def next_row(value):
    return pltpu.roll(value, TILE - 1, 0)


def prev_row(value):
    return pltpu.roll(value, 1, 0)


def build_weights(start, rows, layers, eps, eps_left, eps_right, half, wx, wy, wz, edge):
    tiles = half.shape[1] // TILE
    lanes = half.shape[2]
    slots = half.shape[0]
    below, above = edges()
    for source, first, count in ((eps_left, 0, LEFT), (eps, LEFT, layers), (eps_right, LEFT + layers, slots - LEFT - layers)):

        def copy(layer, carry, source=source, first=first):
            for tile in range(tiles):
                half[first + layer, tile_rows(tile)] = source[layer, window_rows(start, tile)] * 0.5
            return carry

        lax.fori_loop(0, count, copy, 0)
    row = lax.broadcasted_iota(jnp.int32, (TILE, lanes), 0)
    lane = lax.broadcasted_iota(jnp.int32, (TILE, lanes), 1)
    last_row = row == TILE - 1
    lane_inside = jnp.where(lane == lanes - 1, 0.0, 1.0)
    lane_edge = jnp.where(lane == 0, 1.0, 0.0) + jnp.where(lane == lanes - 1, 1.0, 0.0)
    at_low = jnp.where(start == 0, 1.0, 0.0)
    at_high = jnp.where(start + tiles * TILE == rows, 1.0, 0.0)
    low_edge = jnp.where(row == 0, at_low, 0.0)
    high_edge = jnp.where(last_row, at_high, 0.0)

    def one(slot, carry):
        x_open = jnp.where(slot == LEFT - 1, below, jnp.where(slot == LEFT + layers - 1, above, 1)).astype(jnp.float32)
        x_edge = jnp.where(slot == LEFT, 1 - below, 0) + jnp.where(slot == LEFT + layers - 1, 1 - above, 0)
        x_edge = x_edge.astype(jnp.float32)
        here = half[slot, tile_rows(0)]
        down = next_row(here)
        for tile in range(tiles):
            wx[slot, tile_rows(tile)] = (here + half[slot + 1, tile_rows(tile)]) * x_open
            wz[slot, tile_rows(tile)] = (here + next_lane(here)) * lane_inside
            border = lane_edge + x_edge
            if tile == 0:
                border = border + low_edge
            if tile == tiles - 1:
                border = border + high_edge
            edge[slot, tile_rows(tile)] = here * border
            if tile < tiles - 1:
                after = half[slot, tile_rows(tile + 1)]
                after_down = next_row(after)
                wy[slot, tile_rows(tile)] = here + jnp.where(last_row, after_down, down)
                here, down = after, after_down
            else:
                wy[slot, tile_rows(tile)] = jnp.where(last_row, 0.0, here + down)
        return carry

    lax.fori_loop(0, slots - 1, one, 0)


def flux_x(field, pair, slot, tile, wx):
    return wx[slot, tile_rows(tile)] * (field[pair, slot + 1, tile_rows(tile)] - field[pair, slot, tile_rows(tile)])


def sweep(field, pairs, first, stop, weights, carried, visit, finish=None):
    wx, wy, wz, edge = weights
    tiles = wy.shape[1] // TILE
    lanes = wy.shape[2]
    row = lax.broadcasted_iota(jnp.int32, (TILE, lanes), 0)
    first_row = row == 0
    last_row = row == TILE - 1
    for pair in range(pairs):
        for tile in range(tiles):
            carried[pair, tile_rows(tile)] = flux_x(field, pair, first - 1, tile, wx)

    def one(slot, carry):
        for pair in range(pairs):
            here = field[pair, slot, tile_rows(0)]
            down = next_row(here)
            came = jnp.zeros_like(here)
            for tile in range(tiles):
                rows = tile_rows(tile)
                along_x = wx[slot, rows] * (field[pair, slot + 1, rows] - here)
                from_x = carried[pair, rows]
                carried[pair, rows] = along_x
                along_z = wz[slot, rows] * (next_lane(here) - here)
                if tile < tiles - 1:
                    after = field[pair, slot, tile_rows(tile + 1)]
                    after_down = next_row(after)
                    below = jnp.where(last_row, after_down, down)
                else:
                    after, after_down, below = here, down, down
                along_y = wy[slot, rows] * (below - here)
                moved = prev_row(along_y)
                from_y = jnp.where(first_row, came, moved)
                came = moved
                result = ((from_x - along_x) + (from_y - along_y)) + ((prev_lane(along_z) - along_z) + edge[slot, rows] * here)
                visit(pair, slot, tile, here, result)
                here, down = after, after_down
            if finish is not None:
                finish(pair)
        return carry

    lax.fori_loop(first, stop, one, 0)


class Sums:
    def __init__(self, totals, tiles, shares):
        self.totals, self.tiles, self.shares = totals, tiles, shares
        self.held = {}

    def add(self, index, tile, value):
        if tile == 0:
            value = value * self.shares[0]
        if tile == self.tiles - 1:
            value = value * self.shares[1]
        self.held[index] = self.held[index] + value if index in self.held else value

    def flush(self, pair):
        for index, value in self.held.items():
            self.totals[pair, index] = self.totals[pair, index] + value
        self.held = {}


def moments_kernel(pairs, chunks, *refs):
    orbital, eps, eps_left, eps_right = refs[:4]
    refs = refs[4:]
    arrived = [refs[p * len(chunks) : (p + 1) * len(chunks)] for p in range(pairs)]
    refs = refs[pairs * len(chunks) :]
    halos = [refs[2 * p : 2 * p + 2] for p in range(pairs)]
    refs = refs[2 * pairs :]
    sums, basis, half, wx, wy, wz, edge, field, first, second, carried, totals = refs
    layers, rows, lanes = orbital.shape
    window = half.shape[1]
    tiles = window // TILE
    start, _ = roles(rows, window)
    weights = (wx, wy, wz, edge)
    build_weights(start, rows, layers, eps, eps_left, eps_right, half, *weights)
    low = jnp.where(start == 0, 1.0, 0.0)
    own = Sums(totals, tiles, (low, 1.0 - low))
    own_tile = jnp.where(start == 0, 0, 1)
    totals[...] = jnp.zeros_like(totals)
    for pair in range(pairs):
        left, right = halos[pair]
        field[pair, 0:LEFT] = left[...]
        field[pair, LEFT + layers :] = right[...]
        for part, (begin, end) in zip(arrived[pair], chunks):

            def one(layer, carry, part=part, begin=begin, pair=pair):
                for tile in range(tiles):
                    value = (FOUR_PI * orbital[layer, window_rows(start, tile)]) * part[layer - begin, tile_rows(tile)]
                    field[pair, LEFT + layer, tile_rows(tile)] = value
                    own.add(0, tile, value * value)
                own.flush(pair)
                return carry

            lax.fori_loop(begin, end, one, 0)

    def keep_first(pair, slot, tile, value, result):
        first[pair, slot, tile_rows(tile)] = result

    def sum_first(pair, slot, tile, value, result):
        first[pair, slot, tile_rows(tile)] = result
        own.add(1, tile, value * result)
        own.add(2, tile, result * result)

    def keep_second(pair, slot, tile, value, result):
        second[pair, slot, tile_rows(tile)] = result

    def sum_second(pair, slot, tile, value, result):
        second[pair, slot, tile_rows(tile)] = result
        own.add(3, tile, value * result)
        own.add(4, tile, result * result)

    def sum_third(pair, slot, tile, value, result):
        own.add(5, tile, value * result)

    begin, end = LEFT, LEFT + layers
    sweep(field, pairs, begin - 1, begin, weights, carried, keep_first)
    sweep(field, pairs, begin, end, weights, carried, sum_first, own.flush)
    sweep(field, pairs, end, end + 2, weights, carried, keep_first)
    sweep(first, pairs, begin, end, weights, carried, sum_second, own.flush)
    sweep(first, pairs, end, end + 1, weights, carried, keep_second)
    face_sums(second, pairs, begin, end, weights, own)
    lane = lax.broadcasted_iota(jnp.int32, (1, sums.shape[1]), 1)
    line = jnp.zeros((1, sums.shape[1]), jnp.float32)
    for pair in range(pairs):
        for index in range(MOMENTS):
            total = jnp.sum(totals[pair, index])
            line = line + jnp.where(lane == pair * MOMENTS + index, total, 0.0)
    sums[...] = line

    def store(layer, carry):
        for pair in range(pairs):
            for order, source in enumerate((field, first, second)):
                for tile in range(tiles - 1):
                    basis[pair, order, layer, tile_rows(tile)] = source[pair, LEFT + layer, window_rows(own_tile * TILE, tile)]
        return carry

    lax.fori_loop(0, layers, store, 0)


def face_sums(field, pairs, begin, end, weights, own):
    wx, wy, wz, edge = weights
    tiles = wy.shape[1] // TILE
    lanes = wy.shape[2]
    row = lax.broadcasted_iota(jnp.int32, (TILE, lanes), 0)
    last_row = row == TILE - 1

    def one(slot, carry):
        for pair in range(pairs):
            here = field[pair, slot, tile_rows(0)]
            down = next_row(here)
            for tile in range(tiles):
                rows = tile_rows(tile)
                step_x = field[pair, slot + 1, rows] - here
                step_z = next_lane(here) - here
                if tile < tiles - 1:
                    after = field[pair, slot, tile_rows(tile + 1)]
                    after_down = next_row(after)
                    below = jnp.where(last_row, after_down, down)
                else:
                    after, after_down, below = here, down, down
                step_y = below - here
                value = (wx[slot, rows] * step_x * step_x + wy[slot, rows] * step_y * step_y) + (
                    wz[slot, rows] * step_z * step_z + edge[slot, rows] * here * here
                )
                own.add(5, tile, value)
                here, down = after, after_down
            own.flush(pair)
        return carry

    lax.fori_loop(begin, end, one, 0)


def first_output_kernel(pairs, chunks, scalars, basis, *refs):
    arrived = [refs[p * len(chunks) : (p + 1) * len(chunks)] for p in range(pairs)]
    out = refs[-1]
    layers, own_rows, _ = out.shape
    window = arrived[0][0].shape[1]
    low_window = lax.rem(lax.axis_index("blk"), 2)
    skip = (1 - low_window) * TILE
    for index, (begin, end) in enumerate(chunks):

        def one(layer, carry, index=index, begin=begin):
            for tile in range(own_rows // TILE):
                rows = tile_rows(tile)
                total = None
                for pair in range(pairs):
                    potential = (
                        scalars[pair, 0] * basis[pair, 0, layer, rows]
                        + scalars[pair, 1] * basis[pair, 1, layer, rows]
                        + scalars[pair, 2] * basis[pair, 2, layer, rows]
                    )
                    term = potential * arrived[pair][index][layer - begin, window_rows(skip, tile)]
                    total = term if total is None else total + term
                out[layer, rows] = -total
            return carry

        lax.fori_loop(begin, end, one, 0)


def second_output_kernel(pairs, chunks, late_chunks, scalars, orbital, eps, eps_left, eps_right, other, *refs):
    n = len(chunks)
    early = [refs[p * n : (p + 1) * n] for p in range(pairs)]
    refs = refs[pairs * n :]
    n = len(late_chunks)
    late = [refs[p * n : (p + 1) * n] for p in range(pairs)]
    refs = refs[pairs * n :]
    halos = [refs[2 * p : 2 * p + 2] for p in range(pairs)]
    refs = refs[2 * pairs :]
    out, half, wx, wy, wz, edge, whole, field, first, carried = refs
    layers, rows, lanes = orbital.shape
    window = half.shape[1]
    tiles = window // TILE
    late_rows = late[0][0].shape[1]
    shared = window - late_rows
    before, start = roles(rows, window)
    weights = (wx, wy, wz, edge)
    build_weights(start, rows, layers, eps, eps_left, eps_right, half, *weights)
    low = jnp.where(start == 0, 1, 0)
    late_at = (1 - low) * shared
    early_at = low * late_rows
    early_from = (1 - low) * (window - shared)
    for pair in range(pairs):
        left, right = halos[pair]
        field[pair, 0:LEFT] = left[...]
        field[pair, LEFT + layers :] = right[...]
        for part, (begin, end) in zip(early[pair], chunks):

            def take_early(layer, carry, part=part, begin=begin, pair=pair):
                for tile in range(shared // TILE):
                    whole[pair, layer, window_rows(early_at, tile)] = part[layer - begin, window_rows(early_from, tile)]
                return carry

            lax.fori_loop(begin, end, take_early, 0)
        for part, (begin, end) in zip(late[pair], late_chunks):

            def take_late(layer, carry, part=part, begin=begin, pair=pair):
                for tile in range(late_rows // TILE):
                    whole[pair, layer, window_rows(late_at, tile)] = part[layer - begin, tile_rows(tile)]
                return carry

            lax.fori_loop(begin, end, take_late, 0)

        def density(layer, carry, pair=pair):
            for tile in range(tiles):
                value = (FOUR_PI * orbital[layer, window_rows(start, tile)]) * whole[pair, layer, tile_rows(tile)]
                field[pair, LEFT + layer, tile_rows(tile)] = value
            return carry

        lax.fori_loop(0, layers, density, 0)

    def inner(pair, slot, tile, value, result):
        first[pair, slot, tile_rows(tile)] = scalars[pair, 1] * value + scalars[pair, 2] * result

    begin, end = LEFT, LEFT + layers
    sweep(field, pairs, begin - 1, end + 1, weights, carried, inner)

    def outer(pair, slot, tile, value, result):
        rows_ = tile_rows(tile)
        potential = scalars[pair, 0] * field[pair, slot, rows_] + result
        field[pair, slot, rows_] = potential * whole[pair, slot - LEFT, rows_]

    sweep(first, pairs, begin, end, weights, carried, outer)
    own_rows = rows // 2
    own_from = (1 - low) * TILE
    own_at = (1 - low) * own_rows
    other_at = low * own_rows

    def store(layer, carry):
        for tile in range(own_rows // TILE):
            total = field[0, LEFT + layer, window_rows(own_from, tile)]
            for pair in range(1, pairs):
                total = total + field[pair, LEFT + layer, window_rows(own_from, tile)]
            out[layer, window_rows(own_at, tile)] = -total
            out[layer, window_rows(other_at, tile)] = other[layer, tile_rows(tile)]
        return carry

    lax.fori_loop(0, layers, store, 0)


def call(kernel, out_shape, scratch, args, name, in_specs=None, work=4_000_000):
    return pl.pallas_call(
        kernel,
        out_shape=out_shape,
        in_specs=in_specs or [VMEM] * len(args),
        out_specs=jax.tree.map(lambda _: VMEM, out_shape),
        scratch_shapes=scratch,
        compiler_params=pltpu.CompilerParams(vmem_limit_bytes=48 << 20),
        cost_estimate=pl.CostEstimate(flops=work, bytes_accessed=work, transcendentals=0),
        name=name,
    )(*args)


def f32(*shape):
    return jax.ShapeDtypeStruct(shape, jnp.float32)


def buffer(*shape):
    return pltpu.VMEM(shape, jnp.float32)


def weight_scratch(slots, window, lanes):
    return [buffer(slots, window, lanes)] + [buffer(slots - 1, window, lanes)] * 4


def coefficients(moments):
    def inner(left, right, power):
        total = 0.0
        for i, p in enumerate(left):
            for j, q in enumerate(right):
                total = total + (p * q) * moments[..., i + j + power]
        return total

    one = jnp.ones_like(moments[..., 0])
    answer = [0.0 * one] * 3
    residual, direction = [one], [one]
    norm = moments[..., 0]
    for iteration in range(3):
        step = norm / inner(direction, direction, 1)
        answer = [answer[i] + step * direction[i] if i < len(direction) else answer[i] for i in range(3)]
        if iteration == 2:
            break
        applied = [0.0] + [step * p for p in direction]
        residual = residual + [0.0 * one]
        residual = [r - q for r, q in zip(residual, applied)]
        norm_next = inner(residual, residual, 0)
        ratio = norm_next / norm
        direction = direction + [0.0 * one]
        direction = [r + ratio * p for r, p in zip(residual, direction)]
        norm = norm_next
    return jnp.stack(answer, axis=-1)


def per_device(orbitals, dielectric):
    orbital = orbitals[0]
    layers, rows, lanes = orbital.shape
    blks, doms = lax.axis_size("blk"), lax.axis_size("dom")
    own_rows = rows // 2
    window = own_rows + TILE
    rest = rows - window
    slots = LEFT + layers + RIGHT
    start, other_start = roles(rows, window)
    odd = lax.rem(lax.axis_index("blk"), 2)
    pair_up = [(i, i ^ 1) for i in range(blks)]
    forward = [(i, (i + 2 - 4 * (i % 2)) % blks) for i in range(blks)]
    to_above = [(i, i + 1) for i in range(doms - 1)]
    to_below = [(i + 1, i) for i in range(doms - 1)]

    def halo(first, last):
        return lax.ppermute(last, "dom", to_above), lax.ppermute(first, "dom", to_below)

    chunks = ((0, 3), (3, layers - 2), (layers - 2, layers))
    send_first = lax.dynamic_slice_in_dim(orbital, other_start, window, axis=1)
    send_second = lax.dynamic_slice_in_dim(orbital, (1 - odd) * window, rest, axis=1)

    eps_left, eps_right = halo(dielectric[:RIGHT], dielectric[layers - LEFT :])
    near = [lax.ppermute(send_first[a:b], "blk", pair_up) for a, b in chunks]
    far = [lax.ppermute(part, "blk", forward) for part in near]
    late_near = [lax.ppermute(send_second[a:b], "blk", pair_up) for a, b in chunks]
    late_far = [lax.ppermute(part, "blk", forward) for part in late_near]

    mine = lax.dynamic_slice_in_dim(orbital, start, window, axis=1)

    def early_halo(parts):
        return halo(FOUR_PI * mine[:RIGHT] * parts[0], FOUR_PI * mine[layers - LEFT :] * parts[2])

    halos = [*early_halo(near), *early_halo(far)]
    weights = weight_scratch(slots, window, lanes)
    sums, basis = call(
        functools.partial(moments_kernel, 2, chunks),
        (f32(1, 128), f32(2, 3, layers, own_rows, lanes)),
        weights
        + [
            buffer(2, slots, window, lanes),
            buffer(2, slots - 1, window, lanes),
            buffer(2, slots - 2, window, lanes),
            buffer(2, window, lanes),
            buffer(2, MOMENTS, TILE, lanes),
        ],
        [orbital, dielectric, eps_left, eps_right, *near, *far, *halos],
        "moments",
    )
    every = lax.all_to_all(jnp.broadcast_to(sums[None], (blks * doms, 1, 128)), ("blk", "dom"), 0, 0, tiled=True)
    every = jnp.sum(every.reshape(blks, doms, 128), axis=1)
    near_sums = every[:, :MOMENTS]
    far_sums = every[:, MOMENTS : 2 * MOMENTS]
    near_sums = near_sums + near_sums[jnp.array([i ^ 1 for i in range(blks)])]
    far_sums = far_sums + far_sums[jnp.array([(i - 1 + 2 * (i % 2)) % blks for i in range(blks)])]
    scalars = coefficients(jnp.stack([near_sums, far_sums], axis=1))
    scalars = lax.dynamic_index_in_dim(scalars, lax.axis_index("blk"), 0, keepdims=False)

    first_half = call(
        functools.partial(first_output_kernel, 2, chunks),
        f32(layers, own_rows, lanes),
        [],
        [scalars, basis, *near, *far],
        "first_output",
        [SMEM] + [VMEM] * (1 + 2 * len(chunks)),
    )

    mine_late = lax.dynamic_slice_in_dim(orbital, (odd * window), rest, axis=1)
    mine_shared = lax.dynamic_slice_in_dim(orbital, rest, window - rest, axis=1)

    def late_halo(parts, early_parts):
        def product(layer_slice, part, early_part):
            late = FOUR_PI * mine_late[layer_slice] * part
            seam = lax.dynamic_slice_in_dim(early_part, odd * rest, window - rest, axis=1)
            seam = FOUR_PI * mine_shared[layer_slice] * seam
            return jnp.where(odd == 1, jnp.concatenate([seam, late], 1), jnp.concatenate([late, seam], 1))

        low = product(slice(0, 2), parts[0][:2], early_parts[0][:2])
        high = product(slice(layers - LEFT, layers), parts[2], early_parts[2])
        return halo(low, high)

    late_halos = [*late_halo(late_near, near), *late_halo(late_far, far)]
    slots = slots - 1
    out = call(
        functools.partial(second_output_kernel, 2, chunks, chunks),
        f32(layers, rows, lanes),
        weight_scratch(slots, window, lanes)
        + [
            buffer(2, layers, window, lanes),
            buffer(2, slots, window, lanes),
            buffer(2, slots - 1, window, lanes),
            buffer(2, window, lanes),
        ],
        [scalars, orbital, dielectric, eps_left, eps_right, first_half, *near, *far, *late_near, *late_far, *late_halos],
        "second_output",
        [SMEM] + [VMEM] * (5 + 4 * len(chunks) + 4),
    )
    return out[None]


def solution(mesh):
    return jax.shard_map(
        per_device,
        mesh=mesh,
        in_specs=(P("blk", "dom", None, None), P("dom", None, None)),
        out_specs=P("blk", "dom", None, None),
        check_vma=False,
    )
```

time: 249 us -> 126 us (0.51)
  blocking collectives: 84.4 us -> 0 us
  waiting for transfers between devices: 90 us -> 23.9 us
  other arithmetic: 50 us -> 9.2 us
  Pallas kernels: 0 us -> 32.5 us
  starting transfers between devices: 16.8 us -> 46.5 us
  local copies, waits for them, and re-layouts: 1.22 us -> 12.8 us
  between operations: 6.38 us -> 0.25 us
    psum x5 -> x0, blocking collectives: 84.4 us -> none  [the longest x3 47.4 us: squares(): return shaped(lax.psum(local_inner(residual, residual), 'dom'))]
    ppermute x10 -> x22, waiting for transfers between devices: 90 us -> 19.8 us  [the longest x3 10.4 us: per_device(): lax.ppermute(send_second[a:b], 'blk', pair_up)]
    pallas_call x0 -> x3, Pallas kernels: none -> 32.5 us  [call(): pl.pallas_call(kernel, out_shape=out_shape, in_specs=in_specs or [VMEM] *...]
    reduce_sum x5 -> x1, other arithmetic: 25.4 us -> 0.02 us  [per_device(): every = jnp.sum(every.reshape(blks, doms, 128), axis=1)]
    ppermute x10 -> x22, starting transfers between devices: 16.8 us -> 42.3 us  [the longest x5 17.1 us: halo(): lax.ppermute(last, 'dom', to_above)]
    concatenate x4 -> x0, other arithmetic: 11.7 us -> none  [padded_2(): jnp.concatenate([lax.ppermute(tail, axis, [(i, (i + 1) % count) for i in...]
    slice x4 -> x9, local copies, waits for them, and re-layouts: 1.17 us -> 9.79 us  [the longest x2 3.94 us: per_device(): eps_left, eps_right = halo(dielectric[:RIGHT], dielectric[layers - LEFT:])]
    add x2, other arithmetic: 4.37 us -> 0.08 us  [coefficients(): answer[i] + step * direction[i]]
  transfers between devices with their start and end apart: 10 -> 23, of which waited for: 5 -> 7; matrix products, arithmetic and copies ran while one was open for 3% -> 16% of each run, Pallas kernels for 0% -> 15%
where the time goes in v1:
time: 126 us; the launch traced here: 125 us
  starting transfers between devices  46.5 us (37%)
  Pallas kernels  32.5 us (26%)
  waiting for transfers between devices  23.9 us (19%)
  local copies, waits for them, and re-layouts  12.8 us (10%)
  other arithmetic  9.2 us (7%)
    pallas_call x3, Pallas kernels, call(): pl.pallas_call(kernel, out_shape=out_shape, in_specs=in_specs or [VMEM] *...  32.5 us
    ppermute x5, starting transfers between devices, halo(): lax.ppermute(last, 'dom', to_above)  17.1 us
    ppermute x3, waiting for transfers between devices, per_device(): lax.ppermute(send_second[a:b], 'blk', pair_up)  10.4 us
    ppermute x5, starting transfers between devices, halo(): lax.ppermute(first, 'dom', to_below)  6.43 us
    ppermute x3, waiting for transfers between devices, per_device(): near = [lax.ppermute(send_first[a:b], 'blk', pair_up) for a, b in chunks]  5.88 us
    ppermute x3, starting transfers between devices, per_device(): late_far = [lax.ppermute(part, 'blk', forward) for part in late_near]  5.68 us
    ppermute x3, starting transfers between devices, per_device(): near = [lax.ppermute(send_first[a:b], 'blk', pair_up) for a, b in chunks]  5.63 us
    all_to_all x1, starting transfers between devices, per_device(): lax.all_to_all(jnp.broadcast_to(sums[None], (blks * doms, 1, 128)), ('blk...  4.28 us
  transfers between devices with their start and end apart: 23, of which 7 were waited for; matrix products, arithmetic and copies ran while one was open for 16% of the time, Pallas kernels for 15%

profile of v1, /device:TPU:0, one launch (start us, length us, event | category | flops | bytes accessed | tf_op | source)
XLA Modules:
  0.0 125.2 jit_solution(5100180159885474033)
XLA Ops:
  0.0 1.0 dynamic-slice_bitcast_fusion.4
  1.0 3.0 %collective-permute-start.4 = (f32[2,136,256]{2,1,0:T(8,128)S(1)}, f32[2,136,256]{2,1,0:T(8,128)S(1)}, u32[]{:S(2)}, u32[]{:S(2)}) collective-permute-start(f32[2,136,256]{2,1,0:T(8,128)S(1)} %dynamic-slice_bitcast_fusion.4), channel_id=1, source_target_pairs={{0,8},{8,0},{16,24},{24,16},{1,9},{9,1},{17,25},{25,17},{2,10},{10... | collective-permute-start | bytes 835592 | tf_op jit(solution)/shard_map/ppermute | solution.py:464
  4.0 1.9 %dynamic-slice_bitcast_fusion.2 = (f32[3,120,256]{2,1,0:T(8,128)}, f32[3,120,256]{2,1,0:T(8,128)S(1)}) fusion(f32[1,8,256,256]{3,2,1,0:T(8,128)} %param.4, s32[]{:T(128)S(6)} %add.236, s32[]{:T(128)S(6)} %select_n.53), kind=kLoop, calls=%fused_computation.6 | loop fusion | bytes 1474568 | tf_op jit(solution)/shard_map/slice | solution.py:466
  5.9 0.0 collective-permute-start.12
  6.0 1.2 dynamic-slice_bitcast_fusion
  7.1 2.1 %collective-permute-start.2 = (f32[3,136,256]{2,1,0:T(8,128)S(1)}, f32[3,136,256]{2,1,0:T(8,128)S(1)}, u32[]{:S(2)}, u32[]{:S(2)}) collective-permute-start(f32[3,136,256]{2,1,0:T(8,128)S(1)} %get-tuple-element.31), channel_id=1, source_target_pairs={{0,8},{8,0},{16,24},{24,16},{1,9},{9,1},{17,25},{25,17},{2,10},{10... | collective-permute-start | bytes 1253384 | tf_op jit(solution)/shard_map/ppermute | solution.py:464
  9.2 2.3 %collective-permute-done.4.refs_6_.refs_2_ = f32[2,136,256]{2,1,0:T(8,128)S(1)} collective-permute-done((f32[2,136,256]{2,1,0:T(8,128)S(1)}, f32[2,136,256]{2,1,0:T(8,128)S(1)}, u32[]{:S(2)}, u32[]{:S(2)}) %collective-permute-start.4) | collective-permute-done | bytes 278560 | tf_op jit(solution)/shard_map/ppermute | solution.py:464
  11.5 2.0 %collective-permute-start.7 = (f32[2,136,256]{2,1,0:T(8,128)S(1)}, f32[2,136,256]{2,1,0:T(8,128)S(1)}, u32[]{:S(2)}, u32[]{:S(2)}) collective-permute-start(f32[2,136,256]{2,1,0:T(8,128)S(1)} %collective-permute-done.4.refs_6_.refs_2_), channel_id=1, source_target_pairs={{0,16},{8,24},{16,0},{24,8},{1,17},{9,25},{17,1},{25,9},{2,18},{10... | collective-permute-start | bytes 835592 | tf_op jit(solution)/shard_map/ppermute | solution.py:465
  13.6 1.7 %dynamic-slice_bitcast_fusion.5 = f32[2,120,256]{2,1,0:T(8,128)} fusion(f32[1,8,256,256]{3,2,1,0:T(8,128)} %param.4, s32[]{:T(128)S(6)} %add.237, s32[]{:T(128)S(6)} %select_n.53), kind=kLoop, calls=%fused_computation.23 | loop fusion | bytes 491528 | tf_op jit(solution)/shard_map/slice | solution.py:466
  15.2 1.5 %collective-permute-start.14 = (f32[2,120,256]{2,1,0:T(8,128)}, f32[2,120,256]{2,1,0:T(8,128)S(1)}, u32[]{:S(2)}, u32[]{:S(2)}) collective-permute-start(f32[2,120,256]{2,1,0:T(8,128)} %dynamic-slice_bitcast_fusion.5), channel_id=1, source_target_pairs={{0,8},{8,0},{16,24},{24,16},{1,9},{9,1},{17,25},{25,17},{2,10},{10... | collective-permute-start | bytes 737288 | tf_op jit(solution)/shard_map/ppermute | solution.py:466
  16.7 0.5 collective-permute-start.3
  17.3 2.2 %collective-permute-done.12.refs_6_ = f32[3,120,256]{2,1,0:T(8,128)S(1)} collective-permute-done((f32[3,120,256]{2,1,0:T(8,128)S(1)}, f32[3,120,256]{2,1,0:T(8,128)S(1)}, u32[]{:S(2)}, u32[]{:S(2)}) %collective-permute-start.12) | collective-permute-done | bytes 368672 | tf_op jit(solution)/shard_map/ppermute | solution.py:466
  19.4 2.0 %collective-permute-start.15 = (f32[3,120,256]{2,1,0:T(8,128)S(1)}, f32[3,120,256]{2,1,0:T(8,128)S(1)}, u32[]{:S(2)}, u32[]{:S(2)}) collective-permute-start(f32[3,120,256]{2,1,0:T(8,128)S(1)} %collective-permute-done.12.refs_6_), channel_id=1, source_target_pairs={{0,16},{8,24},{16,0},{24,8},{1,17},{9,25},{17,1},{25,9},{2,18},{10... | collective-permute-start | bytes 1105928 | tf_op jit(solution)/shard_map/ppermute | solution.py:467
  21.5 1.9 %slice.130 = f32[2,256,256]{2,1,0:T(8,128)} slice(f32[8,256,256]{2,1,0:T(8,128)} %eps.1), slice={[6:8], [0:256], [0:256]} | slice | bytes 1048576 | tf_op jit(solution)/shard_map/slice | solution.py:463
  23.4 2.1 %slice.131 = f32[3,256,256]{2,1,0:T(8,128)} slice(f32[8,256,256]{2,1,0:T(8,128)} %eps.1), slice={[0:3], [0:256], [0:256]} | slice | bytes 1572864 | tf_op jit(solution)/shard_map/slice | solution.py:463
  25.4 8.2 %collective-permute-done.14.refs_8_ = f32[2,120,256]{2,1,0:T(8,128)S(1)} collective-permute-done((f32[2,120,256]{2,1,0:T(8,128)}, f32[2,120,256]{2,1,0:T(8,128)S(1)}, u32[]{:S(2)}, u32[]{:S(2)}) %collective-permute-start.14) | collective-permute-done | bytes 245792 | tf_op jit(solution)/shard_map/ppermute | solution.py:466
  33.7 1.3 %collective-permute-start.1 = (f32[3,256,256]{2,1,0:T(8,128)}, f32[3,256,256]{2,1,0:T(8,128)S(1)}, u32[]{:S(2)}, u32[]{:S(2)}) collective-permute-start(f32[3,256,256]{2,1,0:T(8,128)} %slice.131), channel_id=1, source_target_pairs={{1,0},{2,1},{3,2},{4,3},{5,4},{6,5},{7,6},{9,8},{10,9},{11,10},{12... | collective-permute-start | bytes 2359304 | tf_op jit(solution)/shard_map/ppermute | solution.py:457
  35.0 2.1 %collective-permute-start.17 = (f32[2,120,256]{2,1,0:T(8,128)S(1)}, f32[2,120,256]{2,1,0:T(8,128)S(1)}, u32[]{:S(2)}, u32[]{:S(2)}) collective-permute-start(f32[2,120,256]{2,1,0:T(8,128)S(1)} %collective-permute-done.14.refs_8_), channel_id=1, source_target_pairs={{0,16},{8,24},{16,0},{24,8},{1,17},{9,25},{17,1},{25,9},{2,18},{10... | collective-permute-start | bytes 737288 | tf_op jit(solution)/shard_map/ppermute | solution.py:467
  37.1 0.1 collective-permute-start.5
  37.2 1.0 fusion.6
  38.2 3.5 %collective-permute-done.3.refs_5_.refs_1_ = f32[3,136,256]{2,1,0:T(8,128)S(1)} collective-permute-done((f32[3,136,256]{2,1,0:T(8,128)S(1)}, f32[3,136,256]{2,1,0:T(8,128)S(1)}, u32[]{:S(2)}, u32[]{:S(2)}) %collective-permute-start.3) | collective-permute-done | bytes 417824 | tf_op jit(solution)/shard_map/ppermute | solution.py:464
  41.8 1.3 %collective-permute-start = (f32[2,256,256]{2,1,0:T(8,128)}, f32[2,256,256]{2,1,0:T(8,128)S(1)}, u32[]{:S(2)}, u32[]{:S(2)}) collective-permute-start(f32[2,256,256]{2,1,0:T(8,128)} %slice.130), channel_id=1, source_target_pairs={{0,1},{1,2},{2,3},{3,4},{4,5},{5,6},{6,7},{8,9},{9,10},{10,11},{11... | collective-permute-start | bytes 1572872 | tf_op jit(solution)/shard_map/ppermute | solution.py:457
  43.1 0.4 collective-permute-done.17.refs_11_
  43.4 2.3 %collective-permute-start.13 = (f32[3,120,256]{2,1,0:T(8,128)}, f32[3,120,256]{2,1,0:T(8,128)}, u32[]{:S(2)}, u32[]{:S(2)}) collective-permute-start(f32[3,120,256]{2,1,0:T(8,128)} %get-tuple-element.24), channel_id=1, source_target_pairs={{0,8},{8,0},{16,24},{24,16},{1,9},{9,1},{17,25},{25,17},{2,10},{10... | collective-permute-start | bytes 1105928 | tf_op jit(solution)/shard_map/ppermute | solution.py:466
  45.7 0.0 collective-permute-done.15.refs_9_
  45.7 1.5 %collective-permute-start.6 = (f32[3,136,256]{2,1,0:T(8,128)S(1)}, f32[3,136,256]{2,1,0:T(8,128)S(1)}, u32[]{:S(2)}, u32[]{:S(2)}) collective-permute-start(f32[3,136,256]{2,1,0:T(8,128)S(1)} %collective-permute-done.3.refs_5_.refs_1_), channel_id=1, source_target_pairs={{0,16},{8,24},{16,0},{24,8},{1,17},{9,25},{17,1},{25,9},{2,18},{10... | collective-permute-start | bytes 1253384 | tf_op jit(solution)/shard_map/ppermute | solution.py:465
  47.2 2.0 %slice_multiply_fusion = (f32[2,120,256]{2,1,0:T(8,128)}, f32[2,120,256]{2,1,0:T(8,128)S(1)}, f32[2,120,256]{2,1,0:T(8,128)S(1)}, f32[2,120,256]{2,1,0:T(8,128)S(1)}) fusion(f32[3,120,256]{2,1,0:T(8,128)S(1)} %collective-permute-done.15.refs_9_, f32[1,8,256,256]{3,2,1,0:T(8,128)} %param.4, s32[]{:T(128)S(6)} %select_n.56, ...), kind=kLoop, calls=%fused_computation.17 | loop fusion | flops 368640 | bytes 2457608 | tf_op jit(solution)/shard_map/mul | solution.py:513
  49.2 3.2 %collective-permute-done.5.refs_7_.refs_3_ = f32[3,136,256]{2,1,0:T(8,128)S(1)} collective-permute-done((f32[3,136,256]{2,1,0:T(8,128)S(1)}, f32[3,136,256]{2,1,0:T(8,128)S(1)}, u32[]{:S(2)}, u32[]{:S(2)}) %collective-permute-start.5) | collective-permute-done | bytes 417824 | tf_op jit(solution)/shard_map/ppermute | solution.py:465
  52.4 1.1 fusion.1
  53.5 1.3 %collective-permute-start.9 = (f32[3,136,256]{2,1,0:T(8,128)S(1)}, f32[3,136,256]{2,1,0:T(8,128)S(1)}, u32[]{:S(2)}, u32[]{:S(2)}) collective-permute-start(f32[3,136,256]{2,1,0:T(8,128)S(1)} %get-tuple-element.27), channel_id=1, source_target_pairs={{1,0},{2,1},{3,2},{4,3},{5,4},{6,5},{7,6},{9,8},{10,9},{11,10},{12... | collective-permute-start | bytes 1253384 | tf_op jit(solution)/shard_map/ppermute | solution.py:457
  54.9 1.3 %collective-permute-start.11 = (f32[3,136,256]{2,1,0:T(8,128)S(1)}, f32[3,136,256]{2,1,0:T(8,128)S(1)}, u32[]{:S(2)}, u32[]{:S(2)}) collective-permute-start(f32[3,136,256]{2,1,0:T(8,128)S(1)} %get-tuple-element.26), channel_id=1, source_target_pairs={{1,0},{2,1},{3,2},{4,3},{5,4},{6,5},{7,6},{9,8},{10,9},{11,10},{12... | collective-permute-start | bytes 1253384 | tf_op jit(solution)/shard_map/ppermute | solution.py:457
  56.2 0.8 dynamic-slice_multiply_fusion.4
  57.0 4.3 %collective-permute-start.8 = (f32[2,136,256]{2,1,0:T(8,128)S(1)}, f32[2,136,256]{2,1,0:T(8,128)S(1)}, u32[]{:S(2)}, u32[]{:S(2)}) collective-permute-start(f32[2,136,256]{2,1,0:T(8,128)S(1)} %get-tuple-element.29), channel_id=1, source_target_pairs={{0,1},{1,2},{2,3},{3,4},{4,5},{5,6},{6,7},{8,9},{9,10},{10,11},{11... | collective-permute-start | bytes 835592 | tf_op jit(solution)/shard_map/ppermute | solution.py:457
  61.2 0.0 collective-permute-done.1.refs_3_.eps_right
  61.3 4.1 %collective-permute-start.10 = (f32[2,136,256]{2,1,0:T(8,128)S(1)}, f32[2,136,256]{2,1,0:T(8,128)S(1)}, u32[]{:S(2)}, u32[]{:S(2)}) collective-permute-start(f32[2,136,256]{2,1,0:T(8,128)S(1)} %get-tuple-element.28), channel_id=1, source_target_pairs={{0,1},{1,2},{2,3},{3,4},{4,5},{5,6},{6,7},{8,9},{9,10},{10,11},{11... | collective-permute-start | bytes 835592 | tf_op jit(solution)/shard_map/ppermute | solution.py:457
  65.4 0.7 maximum_select_fusion
  66.1 0.7 maximum_select_fusion.1
  66.8 0.7 maximum_select_fusion.2
  67.6 0.0 collective-permute-done.6.refs_8_.refs_4_
  67.6 1.5 %collective-permute-start.16 = (f32[3,120,256]{2,1,0:T(8,128)}, f32[3,120,256]{2,1,0:T(8,128)}, u32[]{:S(2)}, u32[]{:S(2)}) collective-permute-start(f32[3,120,256]{2,1,0:T(8,128)} %collective-permute-done.13.refs_7_), channel_id=1, source_target_pairs={{0,16},{8,24},{16,0},{24,8},{1,17},{9,25},{17,1},{25,9},{2,18},{10... | collective-permute-start | bytes 1105928 | tf_op jit(solution)/shard_map/ppermute | solution.py:467
  69.1 0.0 collective-permute-done.8.refs_10_
  69.1 2.9 %collective-permute-start.18 = (f32[2,136,256]{2,1,0:T(8,128)}, f32[2,136,256]{2,1,0:T(8,128)}, u32[]{:S(2)}, u32[]{:S(2)}) collective-permute-start(f32[2,136,256]{2,1,0:T(8,128)} %maximum_select_fusion), channel_id=1, source_target_pairs={{0,1},{1,2},{2,3},{3,4},{4,5},{5,6},{6,7},{8,9},{9,10},{10,11},{11... | collective-permute-start | bytes 835592 | tf_op jit(solution)/shard_map/ppermute | solution.py:457
  71.9 1.3 %collective-permute-start.19 = (f32[2,136,256]{2,1,0:T(8,128)}, f32[2,136,256]{2,1,0:T(8,128)}, u32[]{:S(2)}, u32[]{:S(2)}) collective-permute-start(f32[2,136,256]{2,1,0:T(8,128)} %maximum_select_fusion.1), channel_id=1, source_target_pairs={{1,0},{2,1},{3,2},{4,3},{5,4},{6,5},{7,6},{9,8},{10,9},{11,10},{12... | collective-permute-start | bytes 835592 | tf_op jit(solution)/shard_map/ppermute | solution.py:457
  73.2 4.6 %collective-permute-start.20 = (f32[2,136,256]{2,1,0:T(8,128)}, f32[2,136,256]{2,1,0:T(8,128)}, u32[]{:S(2)}, u32[]{:S(2)}) collective-permute-start(f32[2,136,256]{2,1,0:T(8,128)} %maximum_select_fusion.2), channel_id=1, source_target_pairs={{0,1},{1,2},{2,3},{3,4},{4,5},{5,6},{6,7},{8,9},{9,10},{10,11},{11... | collective-permute-start | bytes 835592 | tf_op jit(solution)/shard_map/ppermute | solution.py:457
  77.8 0.0 collective-permute-done.11.refs_13_
  77.8 15.3 %moments.1 = (f32[1,128]{1,0:T(1,128)S(1)}, f32[2,3,8,128,256]{4,3,2,1,0:T(8,128)}) custom-call(f32[8,256,256]{2,1,0:T(8,128)} %bitcast.51, f32[8,256,256]{2,1,0:T(8,128)} %eps.1, f32[2,256,256]{2,1,0:T(8,128)S(1)} %collective-permute-done.refs_2_.eps_left, f32[3,256,256]{2,1,0:T(8,128)S(1)} %collective-permute-done.1.refs_3_.eps_right, ...), custom_call_target="tpu_custom_call" | custom-call | flops 4000000 | bytes 4000000 | tf_op jit(solution)/shard_map/moments/pallas_call | solution.py:389
  93.1 0.6 broadcast_in_dim.18
  93.7 4.3 %all-to-all-start = ((f32[32,1,128]{2,1,0:T(1,128)}), f32[32,1,128]{2,1,0:T(1,128)S(1)}, u32[]{:S(2)}, u32[]{:S(2)}) async-start(f32[32,1,128]{2,1,0:T(1,128)} %broadcast_in_dim.18), calls=%async_computation | async-start | bytes 32768 | tf_op jit(solution)/shard_map/all_to_all | solution.py:490
  98.0 1.8 %maximum_select_fusion.3 = f32[2,136,256]{2,1,0:T(8,128)} fusion(f32[2,120,256]{2,1,0:T(8,128)} %get-tuple-element.20, f32[2,16,256]{2,1,0:T(8,128)S(1)} %get-tuple-element.16, pred[]{:T(512)S(6)} %eq.2), kind=kLoop, calls=%fused_computation.16 | loop fusion | flops 208896 | bytes 557057 | tf_op jit(solution)/shard_map/jit(_where)/select_n | solution.py:516
  99.8 1.3 %collective-permute-start.21 = (f32[2,136,256]{2,1,0:T(8,128)}, f32[2,136,256]{2,1,0:T(8,128)}, u32[]{:S(2)}, u32[]{:S(2)}) collective-permute-start(f32[2,136,256]{2,1,0:T(8,128)} %maximum_select_fusion.3), channel_id=1, source_target_pairs={{1,0},{2,1},{3,2},{4,3},{5,4},{6,5},{7,6},{9,8},{10,9},{11,10},{12... | collective-permute-start | bytes 835592 | tf_op jit(solution)/shard_map/ppermute | solution.py:457
  101.1 4.1 %all-to-all-done = f32[32,1,128]{2,1,0:T(1,128)S(1)} async-done(((f32[32,1,128]{2,1,0:T(1,128)}), f32[32,1,128]{2,1,0:T(1,128)S(1)}, u32[]{:S(2)}, u32[]{:S(2)}) %all-to-all-start) | async-done | bytes 16416 | tf_op jit(solution)/shard_map/all_to_all | solution.py:490
  105.2 0.1 fusion.30
  105.3 0.6 gather_fusion
  105.8 0.6 gather_fusion.1
  106.4 0.1 add_bitcast_fusion.1
  106.5 0.1 copy.6
  106.6 0.1 copy.5
  106.7 0.1 multiply_add_fusion.1
  106.8 0.1 fusion.10
  106.8 0.1 copy.7
  106.9 3.5 %first_output.1.other = f32[8,128,256]{2,1,0:T(8,128)S(1)} custom-call(f32[2,3]{1,0:T(2,128)S(1)} %bitcast.47, f32[2,3,8,128,256]{4,3,2,1,0:T(8,128)} %get-tuple-element.8.basis, f32[3,136,256]{2,1,0:T(8,128)S(1)} %collective-permute-done.2.refs_4_.refs_0_, f32[3,136,256]{2,1,0:T(8,128)S(1)} %collective-permute-done.3.refs_5_.refs_1_, ...), custom_call_target="tpu_custom_call" | custom-call | flops 4000000 | bytes 4000000 | tf_op jit(solution)/shard_map/first_output/pallas_call | solution.py:389
  110.4 1.0 copy-done
  111.4 0.0 collective-permute-done.16.refs_10_
  111.4 13.7 %second_output.1 = f32[8,256,256]{2,1,0:T(8,128)} custom-call(f32[2,3]{1,0:T(2,128)S(1)} %bitcast.48, f32[8,256,256]{2,1,0:T(8,128)} %bitcast.52, f32[8,256,256]{2,1,0:T(8,128)} %eps.1, f32[2,256,256]{2,1,0:T(8,128)S(1)} %collective-permute-done.refs_2_.eps_left, f32[3,256,256]{2,1,0:T(8,128)} %copy-done.1, f32[8,128,256]{2,1,0:T(8,128)} %copy-done, ...), custom_call_target="tpu_custom_call" | custom-call | flops 4000000 | bytes 4000000 | tf_op jit(solution)/shard_map/second_output/pallas_call | solution.py:389
  (31 shorter events, 0.1 us)
Async XLA Ops:
  0.0 21.5 %copy-start.7 = (s32[4]{0:T(128)S(1)}, s32[4]{0:T(128)}, u32[]{:S(2)}) copy-start(s32[4]{0:T(128)} %constant.54) | copy-start | bytes 52
  1.0 10.5 %collective-permute-start.4 = (f32[2,136,256]{2,1,0:T(8,128)S(1)}, f32[2,136,256]{2,1,0:T(8,128)S(1)}, u32[]{:S(2)}, u32[]{:S(2)}) collective-permute-start(f32[2,136,256]{2,1,0:T(8,128)S(1)} %dynamic-slice_bitcast_fusion.4), channel_id=1, source_target_pairs={{0,8},{8,0},{16,24},{24,16},{1,9},{9,1},{17,25},{25,17},{2,10},{10... | collective-permute-start | bytes 835592 | tf_op jit(solution)/shard_map/ppermute | solution.py:464
  5.9 19.5 %copy-start.6 = (s32[4]{0:T(128)S(1)}, s32[4]{0:T(128)}, u32[]{:S(2)}) copy-start(s32[4]{0:T(128)} %constant.55) | copy-start | bytes 52
  5.9 13.5 %collective-permute-start.12 = (f32[3,120,256]{2,1,0:T(8,128)S(1)}, f32[3,120,256]{2,1,0:T(8,128)S(1)}, u32[]{:S(2)}, u32[]{:S(2)}) collective-permute-start(f32[3,120,256]{2,1,0:T(8,128)S(1)} %get-tuple-element.25), channel_id=1, source_target_pairs={{0,8},{8,0},{16,24},{24,16},{1,9},{9,1},{17,25},{25,17},{2,10},{10... | collective-permute-start | bytes 1105928 | tf_op jit(solution)/shard_map/ppermute | solution.py:466
  7.1 27.8 %collective-permute-start.2 = (f32[3,136,256]{2,1,0:T(8,128)S(1)}, f32[3,136,256]{2,1,0:T(8,128)S(1)}, u32[]{:S(2)}, u32[]{:S(2)}) collective-permute-start(f32[3,136,256]{2,1,0:T(8,128)S(1)} %get-tuple-element.31), channel_id=1, source_target_pairs={{0,8},{8,0},{16,24},{24,16},{1,9},{9,1},{17,25},{25,17},{2,10},{10... | collective-permute-start | bytes 1253384 | tf_op jit(solution)/shard_map/ppermute | solution.py:464
  11.5 25.6 %collective-permute-start.7 = (f32[2,136,256]{2,1,0:T(8,128)S(1)}, f32[2,136,256]{2,1,0:T(8,128)S(1)}, u32[]{:S(2)}, u32[]{:S(2)}) collective-permute-start(f32[2,136,256]{2,1,0:T(8,128)S(1)} %collective-permute-done.4.refs_6_.refs_2_), channel_id=1, source_target_pairs={{0,16},{8,24},{16,0},{24,8},{1,17},{9,25},{17,1},{25,9},{2,18},{10... | collective-permute-start | bytes 835592 | tf_op jit(solution)/shard_map/ppermute | solution.py:465
  15.2 18.4 %collective-permute-start.14 = (f32[2,120,256]{2,1,0:T(8,128)}, f32[2,120,256]{2,1,0:T(8,128)S(1)}, u32[]{:S(2)}, u32[]{:S(2)}) collective-permute-start(f32[2,120,256]{2,1,0:T(8,128)} %dynamic-slice_bitcast_fusion.5), channel_id=1, source_target_pairs={{0,8},{8,0},{16,24},{24,16},{1,9},{9,1},{17,25},{25,17},{2,10},{10... | collective-permute-start | bytes 737288 | tf_op jit(solution)/shard_map/ppermute | solution.py:466
  16.7 25.0 %collective-permute-start.3 = (f32[3,136,256]{2,1,0:T(8,128)S(1)}, f32[3,136,256]{2,1,0:T(8,128)S(1)}, u32[]{:S(2)}, u32[]{:S(2)}) collective-permute-start(f32[3,136,256]{2,1,0:T(8,128)S(1)} %get-tuple-element.30), channel_id=1, source_target_pairs={{0,8},{8,0},{16,24},{24,16},{1,9},{9,1},{17,25},{25,17},{2,10},{10... | collective-permute-start | bytes 1253384 | tf_op jit(solution)/shard_map/ppermute | solution.py:464
  19.4 26.3 %collective-permute-start.15 = (f32[3,120,256]{2,1,0:T(8,128)S(1)}, f32[3,120,256]{2,1,0:T(8,128)S(1)}, u32[]{:S(2)}, u32[]{:S(2)}) collective-permute-start(f32[3,120,256]{2,1,0:T(8,128)S(1)} %collective-permute-done.12.refs_6_), channel_id=1, source_target_pairs={{0,16},{8,24},{16,0},{24,8},{1,17},{9,25},{17,1},{25,9},{2,18},{10... | collective-permute-start | bytes 1105928 | tf_op jit(solution)/shard_map/ppermute | solution.py:467
  33.7 12.1 %copy-start.2 = (f32[2,120,256]{2,1,0:T(8,128)}, f32[2,120,256]{2,1,0:T(8,128)S(1)}, u32[]{:S(2)}) copy-start(f32[2,120,256]{2,1,0:T(8,128)S(1)} %collective-permute-done.14.refs_8_) | copy-start | bytes 737284
  33.7 27.6 %collective-permute-start.1 = (f32[3,256,256]{2,1,0:T(8,128)}, f32[3,256,256]{2,1,0:T(8,128)S(1)}, u32[]{:S(2)}, u32[]{:S(2)}) collective-permute-start(f32[3,256,256]{2,1,0:T(8,128)} %slice.131), channel_id=1, source_target_pairs={{1,0},{2,1},{3,2},{4,3},{5,4},{6,5},{7,6},{9,8},{10,9},{11,10},{12... | collective-permute-start | bytes 2359304 | tf_op jit(solution)/shard_map/ppermute | solution.py:457
  35.0 8.5 %collective-permute-start.17 = (f32[2,120,256]{2,1,0:T(8,128)S(1)}, f32[2,120,256]{2,1,0:T(8,128)S(1)}, u32[]{:S(2)}, u32[]{:S(2)}) collective-permute-start(f32[2,120,256]{2,1,0:T(8,128)S(1)} %collective-permute-done.14.refs_8_), channel_id=1, source_target_pairs={{0,16},{8,24},{16,0},{24,8},{1,17},{9,25},{17,1},{25,9},{2,18},{10... | collective-permute-start | bytes 737288 | tf_op jit(solution)/shard_map/ppermute | solution.py:467
  37.1 15.3 %collective-permute-start.5 = (f32[3,136,256]{2,1,0:T(8,128)S(1)}, f32[3,136,256]{2,1,0:T(8,128)S(1)}, u32[]{:S(2)}, u32[]{:S(2)}) collective-permute-start(f32[3,136,256]{2,1,0:T(8,128)S(1)} %collective-permute-done.2.refs_4_.refs_0_), channel_id=1, source_target_pairs={{0,16},{8,24},{16,0},{24,8},{1,17},{9,25},{17,1},{25,9},{2,18},{10... | collective-permute-start | bytes 1253384 | tf_op jit(solution)/shard_map/ppermute | solution.py:465
  41.8 15.2 %collective-permute-start = (f32[2,256,256]{2,1,0:T(8,128)}, f32[2,256,256]{2,1,0:T(8,128)S(1)}, u32[]{:S(2)}, u32[]{:S(2)}) collective-permute-start(f32[2,256,256]{2,1,0:T(8,128)} %slice.130), channel_id=1, source_target_pairs={{0,1},{1,2},{2,3},{3,4},{4,5},{5,6},{6,7},{8,9},{9,10},{10,11},{11... | collective-permute-start | bytes 1572872 | tf_op jit(solution)/shard_map/ppermute | solution.py:457
  43.4 10.1 %copy-start.4 = (f32[2,120,256]{2,1,0:T(8,128)}, f32[2,120,256]{2,1,0:T(8,128)S(1)}, u32[]{:S(2)}) copy-start(f32[2,120,256]{2,1,0:T(8,128)S(1)} %collective-permute-done.17.refs_11_) | copy-start | bytes 737284
  43.4 11.4 %collective-permute-start.13 = (f32[3,120,256]{2,1,0:T(8,128)}, f32[3,120,256]{2,1,0:T(8,128)}, u32[]{:S(2)}, u32[]{:S(2)}) collective-permute-start(f32[3,120,256]{2,1,0:T(8,128)} %get-tuple-element.24), channel_id=1, source_target_pairs={{0,8},{8,0},{16,24},{24,16},{1,9},{9,1},{17,25},{25,17},{2,10},{10... | collective-permute-start | bytes 1105928 | tf_op jit(solution)/shard_map/ppermute | solution.py:466
  45.7 21.8 %collective-permute-start.6 = (f32[3,136,256]{2,1,0:T(8,128)S(1)}, f32[3,136,256]{2,1,0:T(8,128)S(1)}, u32[]{:S(2)}, u32[]{:S(2)}) collective-permute-start(f32[3,136,256]{2,1,0:T(8,128)S(1)} %collective-permute-done.3.refs_5_.refs_1_), channel_id=1, source_target_pairs={{0,16},{8,24},{16,0},{24,8},{1,17},{9,25},{17,1},{25,9},{2,18},{10... | collective-permute-start | bytes 1253384 | tf_op jit(solution)/shard_map/ppermute | solution.py:465
  53.5 19.7 %collective-permute-start.9 = (f32[3,136,256]{2,1,0:T(8,128)S(1)}, f32[3,136,256]{2,1,0:T(8,128)S(1)}, u32[]{:S(2)}, u32[]{:S(2)}) collective-permute-start(f32[3,136,256]{2,1,0:T(8,128)S(1)} %get-tuple-element.27), channel_id=1, source_target_pairs={{1,0},{2,1},{3,2},{4,3},{5,4},{6,5},{7,6},{9,8},{10,9},{11,10},{12... | collective-permute-start | bytes 1253384 | tf_op jit(solution)/shard_map/ppermute | solution.py:457
  54.9 23.0 %collective-permute-start.11 = (f32[3,136,256]{2,1,0:T(8,128)S(1)}, f32[3,136,256]{2,1,0:T(8,128)S(1)}, u32[]{:S(2)}, u32[]{:S(2)}) collective-permute-start(f32[3,136,256]{2,1,0:T(8,128)S(1)} %get-tuple-element.26), channel_id=1, source_target_pairs={{1,0},{2,1},{3,2},{4,3},{5,4},{6,5},{7,6},{9,8},{10,9},{11,10},{12... | collective-permute-start | bytes 1253384 | tf_op jit(solution)/shard_map/ppermute | solution.py:457
  57.0 12.1 %collective-permute-start.8 = (f32[2,136,256]{2,1,0:T(8,128)S(1)}, f32[2,136,256]{2,1,0:T(8,128)S(1)}, u32[]{:S(2)}, u32[]{:S(2)}) collective-permute-start(f32[2,136,256]{2,1,0:T(8,128)S(1)} %get-tuple-element.29), channel_id=1, source_target_pairs={{0,1},{1,2},{2,3},{3,4},{4,5},{5,6},{6,7},{8,9},{9,10},{10,11},{11... | collective-permute-start | bytes 835592 | tf_op jit(solution)/shard_map/ppermute | solution.py:457
  61.3 31.9 %copy-start.1 = (f32[3,256,256]{2,1,0:T(8,128)}, f32[3,256,256]{2,1,0:T(8,128)S(1)}, u32[]{:S(2)}) copy-start(f32[3,256,256]{2,1,0:T(8,128)S(1)} %collective-permute-done.1.refs_3_.eps_right) | copy-start | bytes 2359300
  61.3 10.7 %collective-permute-start.10 = (f32[2,136,256]{2,1,0:T(8,128)S(1)}, f32[2,136,256]{2,1,0:T(8,128)S(1)}, u32[]{:S(2)}, u32[]{:S(2)}) collective-permute-start(f32[2,136,256]{2,1,0:T(8,128)S(1)} %get-tuple-element.28), channel_id=1, source_target_pairs={{0,1},{1,2},{2,3},{3,4},{4,5},{5,6},{6,7},{8,9},{9,10},{10,11},{11... | collective-permute-start | bytes 835592 | tf_op jit(solution)/shard_map/ppermute | solution.py:457
  67.6 43.8 %collective-permute-start.16 = (f32[3,120,256]{2,1,0:T(8,128)}, f32[3,120,256]{2,1,0:T(8,128)}, u32[]{:S(2)}, u32[]{:S(2)}) collective-permute-start(f32[3,120,256]{2,1,0:T(8,128)} %collective-permute-done.13.refs_7_), channel_id=1, source_target_pairs={{0,16},{8,24},{16,0},{24,8},{1,17},{9,25},{17,1},{25,9},{2,18},{10... | collective-permute-start | bytes 1105928 | tf_op jit(solution)/shard_map/ppermute | solution.py:467
  69.1 42.3 %collective-permute-start.18 = (f32[2,136,256]{2,1,0:T(8,128)}, f32[2,136,256]{2,1,0:T(8,128)}, u32[]{:S(2)}, u32[]{:S(2)}) collective-permute-start(f32[2,136,256]{2,1,0:T(8,128)} %maximum_select_fusion), channel_id=1, source_target_pairs={{0,1},{1,2},{2,3},{3,4},{4,5},{5,6},{6,7},{8,9},{9,10},{10,11},{11... | collective-permute-start | bytes 835592 | tf_op jit(solution)/shard_map/ppermute | solution.py:457
  71.9 39.5 %collective-permute-start.19 = (f32[2,136,256]{2,1,0:T(8,128)}, f32[2,136,256]{2,1,0:T(8,128)}, u32[]{:S(2)}, u32[]{:S(2)}) collective-permute-start(f32[2,136,256]{2,1,0:T(8,128)} %maximum_select_fusion.1), channel_id=1, source_target_pairs={{1,0},{2,1},{3,2},{4,3},{5,4},{6,5},{7,6},{9,8},{10,9},{11,10},{12... | collective-permute-start | bytes 835592 | tf_op jit(solution)/shard_map/ppermute | solution.py:457
  73.2 38.2 %collective-permute-start.20 = (f32[2,136,256]{2,1,0:T(8,128)}, f32[2,136,256]{2,1,0:T(8,128)}, u32[]{:S(2)}, u32[]{:S(2)}) collective-permute-start(f32[2,136,256]{2,1,0:T(8,128)} %maximum_select_fusion.2), channel_id=1, source_target_pairs={{0,1},{1,2},{2,3},{3,4},{4,5},{5,6},{6,7},{8,9},{9,10},{10,11},{11... | collective-permute-start | bytes 835592 | tf_op jit(solution)/shard_map/ppermute | solution.py:457
  93.7 11.5 %all-to-all-start = ((f32[32,1,128]{2,1,0:T(1,128)}), f32[32,1,128]{2,1,0:T(1,128)S(1)}, u32[]{:S(2)}, u32[]{:S(2)}) async-start(f32[32,1,128]{2,1,0:T(1,128)} %broadcast_in_dim.18), calls=%async_computation | async-start | bytes 32768 | tf_op jit(solution)/shard_map/all_to_all | solution.py:490
  99.8 11.6 %collective-permute-start.21 = (f32[2,136,256]{2,1,0:T(8,128)}, f32[2,136,256]{2,1,0:T(8,128)}, u32[]{:S(2)}, u32[]{:S(2)}) collective-permute-start(f32[2,136,256]{2,1,0:T(8,128)} %maximum_select_fusion.3), channel_id=1, source_target_pairs={{1,0},{2,1},{3,2},{4,3},{5,4},{6,5},{7,6},{9,8},{10,9},{11,10},{12... | collective-permute-start | bytes 835592 | tf_op jit(solution)/shard_map/ppermute | solution.py:457
  106.9 4.5 %copy-start.3 = (f32[2,120,256]{2,1,0:T(8,128)S(1)}, f32[2,120,256]{2,1,0:T(8,128)}, u32[]{:S(2)}) copy-start(f32[2,120,256]{2,1,0:T(8,128)} %copy-done.2) | copy-start | bytes 737284
  106.9 4.5 %copy-start.5 = (f32[2,120,256]{2,1,0:T(8,128)S(1)}, f32[2,120,256]{2,1,0:T(8,128)}, u32[]{:S(2)}) copy-start(f32[2,120,256]{2,1,0:T(8,128)} %copy-done.4) | copy-start | bytes 737284
  110.4 1.0 copy-start
